TPU v7x, 32 devices: a whole 2x2x4 slice. The times are simulated.
32 devices in a mesh: ctx: 8 (over z, y), grp: 4 (over x, core).
Axes of the slice: x: 2, y: 2, z: 4, core: 2. Of those that a mesh axis runs over, the one named last changes fastest.
Arguments:
- streams: bfloat16 [3, 3072, 4096], P(None, 'ctx', 'grp'), may hold values from -400 to 400
- filters: bfloat16 [3, 256, 128], P(None, 'grp'), may hold values from -0.5 to 0.5
- gain: float32 [4096], P('grp'), may hold values from 0.5 to 1.5
Outputs:
- normed: bfloat16 [3072, 4096], P('ctx', 'grp')
All inputs are finite; a program needn't handle non-finite values.
Results may differ from a plain program's by a relative error of at most 0.012.
The roundings to bfloat16 on the way count: a program that leaves them out, or rounds other values in their place, can miss the bound.
Values may be sent and summed in bfloat16 or wider, within the bound.
A program may use at most 128 MiB of HBM per device.

v0:
```python
import math
import jax
import jax.numpy as jnp
import numpy as np
from jax import lax
from jax.sharding import PartitionSpec as P

HD = 128
CH = 4096


def passed_along(block, axis, distance):
    devices = range(lax.axis_size(axis))
    route = [(i - distance, i) for i in devices if i - distance in devices]
    return lax.ppermute(block, axis, route)


def filter_all(streams, filters):
    tok_rows = streams.shape[1]
    chan_count = streams.shape[2]
    filt_len = filters.shape[2]
    group_count = filters.shape[1]
    group_width = chan_count // group_count
    tail = streams[:, tok_rows - filt_len :, :]
    before = passed_along(tail, "ctx", 1)
    padded = jnp.concatenate([before, streams], axis=1)
    block_count = tok_rows // filt_len
    blocks = padded.reshape(3, block_count + 1, filt_len, group_count, group_width)
    lag_table = np.arange(filt_len)[:, None] - np.arange(filt_len)[None, :]
    lower_idx = np.where(lag_table >= 0, lag_table, 0)
    upper_idx = np.where(lag_table < 0, lag_table + filt_len, 0)
    lower = jnp.where(lag_table >= 0, filters[:, :, lower_idx], 0.0)
    upper = jnp.where(lag_table < 0, filters[:, :, upper_idx], 0.0)
    result = jnp.einsum(
        "agts,absgc->abtgc", lower, blocks[:, 1:], preferred_element_type=jnp.float32
    )
    result = result + jnp.einsum(
        "agts,absgc->abtgc", upper, blocks[:, :-1], preferred_element_type=jnp.float32
    )
    return result.reshape(3, tok_rows, chan_count).astype(jnp.bfloat16)


def attend(queries, positions, keyed, valued):
    tok_rows, chan_count = queries.shape
    head_count = chan_count // HD
    scale = HD ** (-0.5)
    query_heads = queries.reshape(tok_rows, head_count, HD)
    query_last = jnp.max(positions)
    start_state = (
        jnp.full((head_count, tok_rows), -1e30, jnp.float32),
        jnp.zeros((head_count, tok_rows), jnp.float32),
        jnp.zeros((tok_rows, head_count, HD), jnp.float32),
    )
    key_piece = lax.all_gather(keyed, "ctx", axis=0, tiled=True)
    value_piece = lax.all_gather(valued, "ctx", axis=0, tiled=True)
    piece_len = key_piece.shape[0]
    block_len = math.gcd(piece_len, 512)

    def step_block(step_idx, state):
        offset = step_idx * block_len
        key_block = lax.dynamic_slice_in_dim(key_piece, offset, block_len, 0).reshape(
            block_len, head_count, HD
        )
        value_block = lax.dynamic_slice_in_dim(value_piece, offset, block_len, 0).reshape(
            block_len, head_count, HD
        )
        key_pos = offset + jnp.arange(block_len, dtype=jnp.int32)

        def update_block(inner):
            running, totals, accum = inner
            scores = (
                jnp.einsum(
                    "shd,khd->hsk", query_heads, key_block, preferred_element_type=jnp.float32
                )
                * scale
            )
            causal = key_pos[None, None, :] <= positions[None, :, None]
            newtop = jnp.maximum(running, jnp.max(jnp.where(causal, scores, -1e30), axis=2))
            weights = jnp.where(causal, jnp.exp(scores - newtop[:, :, None]), 0.0)
            factor = jnp.exp(running - newtop)
            totals = totals * factor + jnp.sum(weights, axis=2)
            accum = accum * factor.T[:, :, None] + jnp.einsum(
                "hsk,khd->shd",
                weights.astype(jnp.bfloat16),
                value_block,
                preferred_element_type=jnp.float32,
            )
            return (newtop, totals, accum)

        return lax.cond(offset > query_last, lambda inner: inner, update_block, state)

    running, totals, accum = lax.fori_loop(0, piece_len // block_len, step_block, start_state)
    return (accum / totals.T[:, :, None]).reshape(tok_rows, chan_count).astype(jnp.bfloat16)


def local(streams, filters, gain):
    features = filter_all(streams, filters)
    tok_rows = streams.shape[1]
    my_index = lax.axis_index("ctx")
    queries = features[0]
    positions = my_index * tok_rows + jnp.arange(tok_rows, dtype=jnp.int32)
    attended = attend(queries, positions, features[1], features[2])
    wide = attended.astype(jnp.float32)
    power = lax.psum(jnp.sum(wide * wide, axis=1), "grp") / CH
    return (wide * gain[None, :] * lax.rsqrt(power + 1e-06)[:, None]).astype(jnp.bfloat16)


def solution(mesh):
    placed = (P(None, "ctx", "grp"), P(None, "grp", None), P("grp"))
    return jax.shard_map(
        local, mesh=mesh, in_specs=placed, out_specs=P("ctx", "grp"), check_vma=False
    )
```

profile of v0, /device:TPU:24, one launch (start us, length us, event | category | flops | bytes accessed | tf_op | source)
XLA Modules:
  0.0 568.2 jit_solution(7154377040794997620)
XLA Ops:
  7.7 3.4 collective-permute-start
  13.0 112.9 %gather_fusion.1 = bf16[16384,3,64]{2,1,0:T(4,128)(2,1)} fusion(bf16[3,64,128]{1,0,2:T(4,128)(2,1)S(1)} %copy.17, s32[16384]{0:T(1024)S(1)} %broadcast_clamp_fusion), kind=kCustom, calls=%fused_computation.1 | custom fusion | bytes 12648448 | tf_op jit(solution)/shard_map/gather | solution.py:33
  125.9 17.2 %copy.21 = bf16[128,128,3,64]{1,0,3,2:T(8,128)(2,1)} copy(bf16[128,128,3,64]{3,2,1,0:T(4,128)(2,1)} %bitcast.81) | data formatting | bytes 12582912 | tf_op jit(solution)/shard_map/gather | solution.py:33
  143.1 112.7 %gather_fusion = bf16[16384,3,64]{2,1,0:T(4,128)(2,1)} fusion(bf16[3,64,128]{1,0,2:T(4,128)(2,1)S(1)} %copy.17, s32[16384]{0:T(1024)S(1)} %broadcast_clamp_fusion.1), kind=kCustom, calls=%fused_computation | custom fusion | bytes 12648448 | tf_op jit(solution)/shard_map/gather | solution.py:32
  255.9 17.2 %copy.18 = bf16[128,128,3,64]{1,0,3,2:T(8,128)(2,1)} copy(bf16[128,128,3,64]{3,2,1,0:T(4,128)(2,1)} %bitcast.80) | data formatting | bytes 12582912 | tf_op jit(solution)/shard_map/gather | solution.py:32
  275.2 3.0 copy.15
  278.2 5.7 %reshape.74 = bf16[3,4,128,64,16]{2,1,4,3,0:T(4,128)(2,1)} reshape(bf16[3,512,1024]{1,2,0:T(8,128)(2,1)} %copy.15) | data formatting | bytes 6291456 | tf_op jit(solution)/shard_map/reshape | solution.py:28
  283.9 8.0 %fusion.40 = (bf16[3,3,128,64,16]{2,1,4,3,0:T(4,128)(2,1)}, bf16[3,3,128,64,16]{2,1,4,3,0:T(4,128)(2,1)S(1)}) fusion(bf16[3,4,128,64,16]{2,1,4,3,0:T(4,128)(2,1)} %reshape.74), kind=kLoop, calls=%fused_computation.56 | loop fusion | bytes 9437184 | tf_op jit(solution)/shard_map/slice | solution.py:35
  292.0 6.0 %fusion.18 = f32[3,64,3,16,128]{4,3,2,1,0:T(8,128)} fusion(bf16[128,128,3,64]{1,0,3,2:T(8,128)(2,1)S(1)} %bitcast.79, pred[128,128]{1,0:T(8,128)(4,1)S(1)} %bitcast.89, bf16[3,3,128,64,16]{2,1,4,3,0:T(4,128)(2,1)S(1)} %get-tuple-element.351), kind=kOutput, calls=%fused_computation.26 | convolution fusion | flops 305135616 | bytes 13385728 | tf_op jit(solution)/shard_map/agts,absgc->abtgc/dot_general | solution.py:37
  298.1 7.8 %fusion.28 = bf16[3,3,128,64,16]{2,4,1,3,0:T(8,128)(2,1)S(1)} fusion(f32[3,64,3,16,128]{4,3,2,1,0:T(8,128)} %fusion.18, bf16[128,128,3,64]{1,0,3,2:T(8,128)(2,1)S(1)} %bitcast.77, pred[128,128]{1,0:T(8,128)(4,1)S(1)} %bitcast.88, bf16[3,3,128,64,16]{2,1,4,3,0:T(4,128)(2,1)} %get-tuple-element.350), kind=kOutput, calls=%fused_computation.38 | convolution fusion | flops 307494912 | bytes 15745024 | tf_op jit(solution)/shard_map/agts,absgc->abtgc/dot_general | solution.py:34
  312.0 93.6 %all-gather.3.cloned.1.call-done = bf16[3072,1024]{0,1:T(8,128)(2,1)} async-done(((bf16[384,1024]{0,1:T(8,128)(2,1)}), bf16[3072,1024]{0,1:T(8,128)(2,1)}) %all-gather.3.cloned.1.call-update) | async-done | bytes 6291472 | tf_op jit(solution)/shard_map/all_gather | solution.py:54
  405.6 99.8 %all-gather.5.cloned.1.call-done = bf16[3072,1024]{0,1:T(8,128)(2,1)} async-done(((bf16[384,1024]{0,1:T(8,128)(2,1)}), bf16[3072,1024]{0,1:T(8,128)(2,1)}) %all-gather.5.cloned.1.call-update) | async-done | bytes 6291472 | tf_op jit(solution)/shard_map/all_gather | solution.py:55
  505.5 47.3 %while.18 = (s32[]{:T(128)}, f32[8,384]{1,0:T(8,128)S(1)}, f32[8,384]{1,0:T(8,128)S(1)}, f32[384,8,128]{2,0,1:T(8,128)S(1)}, s32[]{:T(128)}, /*index=5*/bf16[307...) while((s32[]{:T(128)}, f32[8,384]{1,0:T(8,128)S(1)}, ...), condition=%wide.region_6.7_spmd.clone, body=%wide.region_1.6_spmd.clone.sunk | while | flops 823601024 | bytes 30095668 | solution.py:92
  506.2 7.3 %conditional.3 = (f32[8,384]{1,0:T(8,128)S(1)}, f32[8,384]{1,0:T(8,128)S(1)}, f32[384,8,128]{2,0,1:T(8,128)S(1)}) conditional(s32[]{:T(128)} %convert_element_type.65, (s32[]{:T(128)}, s32[512]{0:T(512)S(1)}, s32[]{:T(128)}, bf16[3072,1024]{0,1:T(8,128)(2,1)}, bf16[384,8,128]{2,0,1:T(8,128)(2,1)S(1)}, /*index=5*/f32[8,384]{1,0:T(8,128)S(1)}, ...), branch_computations={%region_2.4_spmd, %region_5.5_spmd} | conditional | flops 823601024 | bytes 30067270 | solution.py:90
  509.6 2.5 bitcast_add_fusion
  514.0 7.3 %conditional.3 = (f32[8,384]{1,0:T(8,128)S(1)}, f32[8,384]{1,0:T(8,128)S(1)}, f32[384,8,128]{2,0,1:T(8,128)S(1)}) conditional(s32[]{:T(128)} %convert_element_type.65, (s32[]{:T(128)}, s32[512]{0:T(512)S(1)}, s32[]{:T(128)}, bf16[3072,1024]{0,1:T(8,128)(2,1)}, bf16[384,8,128]{2,0,1:T(8,128)(2,1)S(1)}, /*index=5*/f32[8,384]{1,0:T(8,128)S(1)}, ...), branch_computations={%region_2.4_spmd, %region_5.5_spmd} | conditional | flops 823601024 | bytes 30067270 | solution.py:90
  517.5 2.5 bitcast_add_fusion
  521.9 7.3 %conditional.3 = (f32[8,384]{1,0:T(8,128)S(1)}, f32[8,384]{1,0:T(8,128)S(1)}, f32[384,8,128]{2,0,1:T(8,128)S(1)}) conditional(s32[]{:T(128)} %convert_element_type.65, (s32[]{:T(128)}, s32[512]{0:T(512)S(1)}, s32[]{:T(128)}, bf16[3072,1024]{0,1:T(8,128)(2,1)}, bf16[384,8,128]{2,0,1:T(8,128)(2,1)S(1)}, /*index=5*/f32[8,384]{1,0:T(8,128)S(1)}, ...), branch_computations={%region_2.4_spmd, %region_5.5_spmd} | conditional | flops 823601024 | bytes 30067270 | solution.py:90
  529.8 7.3 %conditional.3 = (f32[8,384]{1,0:T(8,128)S(1)}, f32[8,384]{1,0:T(8,128)S(1)}, f32[384,8,128]{2,0,1:T(8,128)S(1)}) conditional(s32[]{:T(128)} %convert_element_type.65, (s32[]{:T(128)}, s32[512]{0:T(512)S(1)}, s32[]{:T(128)}, bf16[3072,1024]{0,1:T(8,128)(2,1)}, bf16[384,8,128]{2,0,1:T(8,128)(2,1)S(1)}, /*index=5*/f32[8,384]{1,0:T(8,128)S(1)}, ...), branch_computations={%region_2.4_spmd, %region_5.5_spmd} | conditional | flops 823601024 | bytes 30067270 | solution.py:90
  537.7 7.3 %conditional.3 = (f32[8,384]{1,0:T(8,128)S(1)}, f32[8,384]{1,0:T(8,128)S(1)}, f32[384,8,128]{2,0,1:T(8,128)S(1)}) conditional(s32[]{:T(128)} %convert_element_type.65, (s32[]{:T(128)}, s32[512]{0:T(512)S(1)}, s32[]{:T(128)}, bf16[3072,1024]{0,1:T(8,128)(2,1)}, bf16[384,8,128]{2,0,1:T(8,128)(2,1)S(1)}, /*index=5*/f32[8,384]{1,0:T(8,128)S(1)}, ...), branch_computations={%region_2.4_spmd, %region_5.5_spmd} | conditional | flops 823601024 | bytes 30067270 | solution.py:90
  541.1 2.5 bitcast_add_fusion
  545.6 7.3 %conditional.3 = (f32[8,384]{1,0:T(8,128)S(1)}, f32[8,384]{1,0:T(8,128)S(1)}, f32[384,8,128]{2,0,1:T(8,128)S(1)}) conditional(s32[]{:T(128)} %convert_element_type.65, (s32[]{:T(128)}, s32[512]{0:T(512)S(1)}, s32[]{:T(128)}, bf16[3072,1024]{0,1:T(8,128)(2,1)}, bf16[384,8,128]{2,0,1:T(8,128)(2,1)S(1)}, /*index=5*/f32[8,384]{1,0:T(8,128)S(1)}, ...), branch_computations={%region_2.4_spmd, %region_5.5_spmd} | conditional | flops 823601024 | bytes 30067270 | solution.py:90
  549.0 2.5 bitcast_add_fusion
  553.4 6.8 %psum.7 = f32[384]{0:T(512)S(1)} all-reduce(f32[384]{0:T(512)S(1)} %get-tuple-element.344), channel_id=1, replica_groups=mesh['ctx'=8,'grp'=4] {'grp'}, use_global_device_ids=true, to_apply=%region_8.9 | all-reduce | flops 384 | bytes 3072 | tf_op jit(solution)/shard_map/psum | solution.py:104
  (111 shorter events, 46.2 us)
Async XLA Ops:
  6.5 399.1 %all-gather.3.cloned.1.call-start = ((), (), s32[]{:S(2)}) async-start(), calls=%async_computation | async-start | bytes 7077888 | tf_op jit(solution)/shard_map/all_gather | solution.py:54
  7.7 265.4 %collective-permute-start = (bf16[3,128,1024]{2,1,0:T(8,128)(2,1)S(1)}, bf16[3,128,1024]{2,1,0:T(8,128)(2,1)}, u32[]{:S(2)}, u32[]{:S(2)}) collective-permute-start(bf16[3,128,1024]{2,1,0:T(8,128)(2,1)S(1)} %slice.21), channel_id=1, source_target_pairs={{0,4},{4,8},{8,12},{12,16},{16,20},{20,24},{24,28},{1,5},{5,9},{9,... | collective-permute-start | bytes 2359304 | tf_op jit(solution)/shard_map/ppermute | solution.py:15
  125.9 17.3 %copy-start.2 = (s32[16384]{0:T(1024)S(1)}, s32[16384]{0:T(1024)}, u32[]{:S(2)}) copy-start(s32[16384]{0:T(1024)} %constant.103) | copy-start | bytes 196612
  278.2 13.7 %slice-start.2 = ((s8[6291456]{0:T(1024)(128)(4,1)}), s8[2097152]{0:T(1024)(128)(4,1)S(1)}, s32[]{:S(2)}) async-start(s8[6291456]{0:T(1024)(128)(4,1)} %bitcast.78), calls=%async_computation.4 | async-start | bytes 4194304
  283.9 8.1 %slice-start.3 = ((s8[6291456]{0:T(1024)(128)(4,1)}), s8[4194304]{0:T(1024)(128)(4,1)S(1)}, s32[]{:S(2)}) async-start(s8[6291456]{0:T(1024)(128)(4,1)} %bitcast.78), calls=%async_computation.5 | async-start | bytes 8388608
  283.9 8.1 %copy-start.1 = (pred[128,128]{1,0:T(32,128)(4,1)S(1)}, pred[128,128]{1,0:T(32,128)(4,1)}, u32[]{:S(2)}) copy-start(pred[128,128]{1,0:T(32,128)(4,1)} %constant.100.clone) | copy-start | bytes 49156
  283.9 14.1 %slice-start = ((s8[6291456]{0:T(1024)(128)(4,1)}), s8[4194304]{0:T(1024)(128)(4,1)S(1)}, s32[]{:S(2)}) async-start(s8[6291456]{0:T(1024)(128)(4,1)} %bitcast.76), calls=%async_computation.2 | async-start | bytes 8388608
  292.0 6.1 %slice-start.1 = ((s8[6291456]{0:T(1024)(128)(4,1)}), s8[2097152]{0:T(1024)(128)(4,1)S(1)}, s32[]{:S(2)}) async-start(s8[6291456]{0:T(1024)(128)(4,1)} %bitcast.76), calls=%async_computation.3 | async-start | bytes 4194304
  292.0 6.1 %copy-start = (pred[128,128]{1,0:T(32,128)(4,1)S(1)}, pred[128,128]{1,0:T(32,128)(4,1)}, u32[]{:S(2)}) copy-start(pred[128,128]{1,0:T(32,128)(4,1)} %constant.98.clone) | copy-start | bytes 49156
  307.9 197.5 %all-gather.5.cloned.1.call-start = ((), (), s32[]{:S(2)}) async-start(), calls=%async_computation.1 | async-start | bytes 7077888 | tf_op jit(solution)/shard_map/all_gather | solution.py:55
  505.5 54.7 %copy-start.3 = (f32[1024]{0:T(1024)S(1)}, f32[1024]{0:T(1024)}, u32[]{:S(2)}) copy-start(f32[1024]{0:T(1024)} %param.15) | copy-start | bytes 12292
Sparse Core Ops, SparseCore 0:
  308.0 97.6 all-gather.2
  407.7 97.6 all-gather.4
where the time goes:
time: 570 us; the launch traced here: 568 us
  local copies, waits for them, and re-layouts  294 us (52%)
  waiting for transfers between devices  193 us (34%)
  matrix products  37.7 us (7%)
  other arithmetic  14.4 us (3%)
  between operations  13.6 us (2%)
  blocking collectives  6.84 us (1%)
    gather x2, local copies, waits for them, and re-layouts, filter_all(): upper = jnp.where(lag_table < 0, filters[:, :, upper_idx], 0.0)  130 us
    gather x2, local copies, waits for them, and re-layouts, filter_all(): lower = jnp.where(lag_table >= 0, filters[:, :, lower_idx], 0.0)  130 us
    all_gather x1, waiting for transfers between devices, attend(): value_piece = lax.all_gather(valued, 'ctx', axis=0, tiled=True)  99.8 us
    all_gather x1, waiting for transfers between devices, attend(): key_piece = lax.all_gather(keyed, 'ctx', axis=0, tiled=True)  93.6 us
    dot_general x6, matrix products, update_block(): jnp.einsum('hsk,khd->shd', weights.astype(jnp.bfloat16), value_block, pre...  14.9 us
  transfers between devices with their start and end apart: 3, of which 2 were waited for; matrix products, arithmetic and copies ran while one was open for 47% of the time, Pallas kernels for 0%

commit v1 on v0

--- a/solution.py
+++ b/solution.py
@@ -52,7 +52,14 @@
         jnp.zeros((tok_rows, head_count, HD), jnp.float32),
     )
     key_piece = lax.all_gather(keyed, "ctx", axis=0, tiled=True)
-    value_piece = lax.all_gather(valued, "ctx", axis=0, tiled=True)
+    ways = lax.axis_size("ctx")
+    pieces = [valued]
+    for far in range(1, ways):
+        pieces.append(
+            lax.ppermute(pieces[far - 1], "ctx", [(d, (d - 1) % ways) for d in range(ways)])
+        )
+    line = jnp.concatenate(pieces, axis=0)
+    value_piece = jnp.roll(line, lax.axis_index("ctx") * valued.shape[0], axis=0)
     piece_len = key_piece.shape[0]
     block_len = math.gcd(piece_len, 512)
 

time: 570 us -> 602 us (1.056)
  local copies, waits for them, and re-layouts: 294 us -> 326 us
  waiting for transfers between devices: 193 us -> 174 us
  starting transfers between devices: 3.65 us -> 21.4 us
    ppermute x0 -> x7, waiting for transfers between devices: none -> 174 us  [attend(): lax.ppermute(pieces[far - 1], 'ctx', [(d, (d - 1) % ways) for d in range(...]
    all_gather x1 -> x0, waiting for transfers between devices: 99.8 us -> none  [attend(): value_piece = lax.all_gather(valued, 'ctx', axis=0, tiled=True)]
    all_gather x1, waiting for transfers between devices: 93.6 us -> 0.01 us  [attend(): key_piece = lax.all_gather(keyed, 'ctx', axis=0, tiled=True)]
    unnamed x20 -> x46, local copies, waits for them, and re-layouts: 3.46 us -> 26.9 us
    ppermute x0 -> x7, starting transfers between devices: none -> 17.9 us  [attend(): lax.ppermute(pieces[far - 1], 'ctx', [(d, (d - 1) % ways) for d in range(...]
    dynamic_slice x0 -> x1, local copies, waits for them, and re-layouts: none -> 8.63 us  [attend(): jnp.roll(line, lax.axis_index('ctx') * valued.shape[0], axis=0)]
  transfers between devices with their start and end apart: 3 -> 9, of which waited for: 2 -> 7; matrix products, arithmetic and copies ran while one was open for 47% -> 50% of each run, Pallas kernels for 0% -> 0%
where the time goes in v1:
time: 602 us; the launch traced here: 597 us
  local copies, waits for them, and re-layouts  326 us (54%)
  waiting for transfers between devices  174 us (29%)
  matrix products  37.7 us (6%)
  starting transfers between devices  21.4 us (4%)
  other arithmetic  14.4 us (2%)
  between operations  13.6 us (2%)
    ppermute x7, waiting for transfers between devices, attend(): lax.ppermute(pieces[far - 1], 'ctx', [(d, (d - 1) % ways) for d in range(...  174 us
    gather x2, local copies, waits for them, and re-layouts, filter_all(): upper = jnp.where(lag_table < 0, filters[:, :, upper_idx], 0.0)  130 us
    gather x2, local copies, waits for them, and re-layouts, filter_all(): lower = jnp.where(lag_table >= 0, filters[:, :, lower_idx], 0.0)  129 us
    unnamed x46, local copies, waits for them, and re-layouts  26.9 us
    ppermute x7, starting transfers between devices, attend(): lax.ppermute(pieces[far - 1], 'ctx', [(d, (d - 1) % ways) for d in range(...  17.9 us
    dot_general x6, matrix products, update_block(): jnp.einsum('hsk,khd->shd', weights.astype(jnp.bfloat16), value_block, pre...  14.9 us
  transfers between devices with their start and end apart: 9, of which 7 were waited for; matrix products, arithmetic and copies ran while one was open for 50% of the time, Pallas kernels for 0%

profile of v1, /device:TPU:24, one launch (start us, length us, event | category | flops | bytes accessed | tf_op | source)
XLA Modules:
  0.0 597.2 jit_solution(15262117205556679872)
XLA Ops:
  13.0 112.3 %gather_fusion.1 = bf16[16384,3,64]{2,1,0:T(4,128)(2,1)} fusion(bf16[3,64,128]{1,0,2:T(4,128)(2,1)S(1)} %copy.17, s32[16384]{0:T(1024)S(1)} %broadcast_clamp_fusion), kind=kCustom, calls=%fused_computation.1 | custom fusion | bytes 12648448 | tf_op jit(solution)/shard_map/gather | solution.py:33
  125.2 17.3 %copy.21 = bf16[128,128,3,64]{1,0,3,2:T(8,128)(2,1)} copy(bf16[128,128,3,64]{3,2,1,0:T(4,128)(2,1)} %bitcast.81) | data formatting | bytes 12582912 | tf_op jit(solution)/shard_map/gather | solution.py:33
  142.5 112.1 %gather_fusion = bf16[16384,3,64]{2,1,0:T(4,128)(2,1)} fusion(bf16[3,64,128]{1,0,2:T(4,128)(2,1)S(1)} %copy.17, s32[16384]{0:T(1024)S(1)} %broadcast_clamp_fusion.1), kind=kCustom, calls=%fused_computation | custom fusion | bytes 12648448 | tf_op jit(solution)/shard_map/gather | solution.py:32
  254.6 17.2 %copy.18 = bf16[128,128,3,64]{1,0,3,2:T(8,128)(2,1)} copy(bf16[128,128,3,64]{3,2,1,0:T(4,128)(2,1)} %bitcast.80) | data formatting | bytes 12582912 | tf_op jit(solution)/shard_map/gather | solution.py:32
  276.9 5.6 reshape.74
  282.5 8.1 %fusion.40 = (bf16[3,3,128,64,16]{2,1,4,3,0:T(4,128)(2,1)}, bf16[3,3,128,64,16]{2,1,4,3,0:T(4,128)(2,1)S(1)}) fusion(bf16[3,4,128,64,16]{2,1,4,3,0:T(4,128)(2,1)} %reshape.74), kind=kLoop, calls=%fused_computation.73 | loop fusion | bytes 9437184 | tf_op jit(solution)/shard_map/slice | solution.py:35
  290.6 6.0 %fusion.18 = f32[3,64,3,16,128]{4,3,2,1,0:T(8,128)} fusion(bf16[128,128,3,64]{1,0,3,2:T(8,128)(2,1)S(1)} %bitcast.79, pred[128,128]{1,0:T(8,128)(4,1)S(1)} %bitcast.88, bf16[3,3,128,64,16]{2,1,4,3,0:T(4,128)(2,1)S(1)} %get-tuple-element.353), kind=kOutput, calls=%fused_computation.26 | convolution fusion | flops 305135616 | bytes 13385728 | tf_op jit(solution)/shard_map/agts,absgc->abtgc/dot_general | solution.py:37
  296.7 7.8 %fusion.28 = bf16[3,3,128,64,16]{2,4,1,3,0:T(8,128)(2,1)S(1)} fusion(f32[3,64,3,16,128]{4,3,2,1,0:T(8,128)} %fusion.18, bf16[128,128,3,64]{1,0,3,2:T(8,128)(2,1)S(1)} %bitcast.77, pred[128,128]{1,0:T(8,128)(4,1)S(1)} %bitcast.87, bf16[3,3,128,64,16]{2,1,4,3,0:T(4,128)(2,1)} %get-tuple-element.352), kind=kOutput, calls=%fused_computation.38 | convolution fusion | flops 307494912 | bytes 15745024 | tf_op jit(solution)/shard_map/agts,absgc->abtgc/dot_general | solution.py:34
  309.6 26.0 %collective-permute-done.1 = bf16[384,1024]{0,1:T(8,128)(2,1)S(1)} collective-permute-done((bf16[384,1024]{0,1:T(8,128)(2,1)S(1)}, bf16[384,1024]{0,1:T(8,128)(2,1)S(1)}, u32[]{:S(2)}, u32[]{:S(2)}) %collective-permute-start.1) | collective-permute-done | bytes 786464 | tf_op jit(solution)/shard_map/ppermute | solution.py:59
  337.9 30.9 %collective-permute-done.2 = bf16[384,1024]{0,1:T(8,128)(2,1)S(1)} collective-permute-done((bf16[384,1024]{0,1:T(8,128)(2,1)S(1)}, bf16[384,1024]{0,1:T(8,128)(2,1)S(1)}, u32[]{:S(2)}, u32[]{:S(2)}) %collective-permute-start.2) | collective-permute-done | bytes 786464 | tf_op jit(solution)/shard_map/ppermute | solution.py:59
  372.2 32.1 %collective-permute-done.3 = bf16[384,1024]{0,1:T(8,128)(2,1)S(1)} collective-permute-done((bf16[384,1024]{0,1:T(8,128)(2,1)S(1)}, bf16[384,1024]{0,1:T(8,128)(2,1)S(1)}, u32[]{:S(2)}, u32[]{:S(2)}) %collective-permute-start.3) | collective-permute-done | bytes 786464 | tf_op jit(solution)/shard_map/ppermute | solution.py:59
  408.6 30.9 %collective-permute-done.4 = bf16[384,1024]{0,1:T(8,128)(2,1)S(1)} collective-permute-done((bf16[384,1024]{0,1:T(8,128)(2,1)S(1)}, bf16[384,1024]{0,1:T(8,128)(2,1)S(1)}, u32[]{:S(2)}, u32[]{:S(2)}) %collective-permute-start.4) | collective-permute-done | bytes 786464 | tf_op jit(solution)/shard_map/ppermute | solution.py:59
  443.8 28.6 %collective-permute-done.5 = bf16[384,1024]{0,1:T(8,128)(2,1)} collective-permute-done((bf16[384,1024]{0,1:T(8,128)(2,1)S(1)}, bf16[384,1024]{0,1:T(8,128)(2,1)}, u32[]{:S(2)}, u32[]{:S(2)}) %collective-permute-start.5) | collective-permute-done | bytes 786464 | tf_op jit(solution)/shard_map/ppermute | solution.py:59
  478.3 16.2 %collective-permute-done.6 = bf16[384,1024]{0,1:T(8,128)(2,1)} collective-permute-done((bf16[384,1024]{0,1:T(8,128)(2,1)}, bf16[384,1024]{0,1:T(8,128)(2,1)}, u32[]{:S(2)}, u32[]{:S(2)}) %collective-permute-start.6) | collective-permute-done | bytes 786464 | tf_op jit(solution)/shard_map/ppermute | solution.py:59
  506.0 8.8 %collective-permute-done.7 = bf16[384,1024]{0,1:T(8,128)(2,1)S(1)} collective-permute-done((bf16[384,1024]{0,1:T(8,128)(2,1)}, bf16[384,1024]{0,1:T(8,128)(2,1)S(1)}, u32[]{:S(2)}, u32[]{:S(2)}) %collective-permute-start.7) | collective-permute-done | bytes 786464 | tf_op jit(solution)/shard_map/ppermute | solution.py:59
  526.5 8.6 %constant_dynamic-slice_fusion.2 = bf16[3072,1024]{0,1:T(8,128)(2,1)} fusion(bf16[6144,1024]{0,1:T(8,128)(2,1)} %constant_dynamic-update-slice_fusion, s32[]{:T(128)S(6)} %select_n.54), kind=kLoop, calls=%fused_computation.70 | loop fusion | bytes 12582916 | tf_op jit(solution)/shard_map/jit(_roll_dynamic)/dynamic_slice | solution.py:62
  535.3 47.7 %while.18 = (s32[]{:T(128)}, f32[8,384]{1,0:T(8,128)S(1)}, f32[8,384]{1,0:T(8,128)S(1)}, f32[384,8,128]{2,0,1:T(8,128)S(1)}, s32[]{:T(128)}, /*index=5*/bf16[307...) while((s32[]{:T(128)}, f32[8,384]{1,0:T(8,128)S(1)}, ...), condition=%wide.region_6.7_spmd.clone, body=%wide.region_1.6_spmd.clone.sunk | while | flops 823601024 | bytes 30095668 | solution.py:99
  536.0 7.3 %conditional.3 = (f32[8,384]{1,0:T(8,128)S(1)}, f32[8,384]{1,0:T(8,128)S(1)}, f32[384,8,128]{2,0,1:T(8,128)S(1)}) conditional(s32[]{:T(128)} %convert_element_type.65, (s32[]{:T(128)}, s32[512]{0:T(512)S(1)}, s32[]{:T(128)}, bf16[3072,1024]{0,1:T(8,128)(2,1)}, bf16[384,8,128]{2,0,1:T(8,128)(2,1)S(1)}, /*index=5*/f32[8,384]{1,0:T(8,128)S(1)}, ...), branch_computations={%region_2.4_spmd, %region_5.5_spmd} | conditional | flops 823601024 | bytes 30067270 | solution.py:97
  543.9 7.3 %conditional.3 = (f32[8,384]{1,0:T(8,128)S(1)}, f32[8,384]{1,0:T(8,128)S(1)}, f32[384,8,128]{2,0,1:T(8,128)S(1)}) conditional(s32[]{:T(128)} %convert_element_type.65, (s32[]{:T(128)}, s32[512]{0:T(512)S(1)}, s32[]{:T(128)}, bf16[3072,1024]{0,1:T(8,128)(2,1)}, bf16[384,8,128]{2,0,1:T(8,128)(2,1)S(1)}, /*index=5*/f32[8,384]{1,0:T(8,128)S(1)}, ...), branch_computations={%region_2.4_spmd, %region_5.5_spmd} | conditional | flops 823601024 | bytes 30067270 | solution.py:97
  551.9 7.3 %conditional.3 = (f32[8,384]{1,0:T(8,128)S(1)}, f32[8,384]{1,0:T(8,128)S(1)}, f32[384,8,128]{2,0,1:T(8,128)S(1)}) conditional(s32[]{:T(128)} %convert_element_type.65, (s32[]{:T(128)}, s32[512]{0:T(512)S(1)}, s32[]{:T(128)}, bf16[3072,1024]{0,1:T(8,128)(2,1)}, bf16[384,8,128]{2,0,1:T(8,128)(2,1)S(1)}, /*index=5*/f32[8,384]{1,0:T(8,128)S(1)}, ...), branch_computations={%region_2.4_spmd, %region_5.5_spmd} | conditional | flops 823601024 | bytes 30067270 | solution.py:97
  559.8 7.3 %conditional.3 = (f32[8,384]{1,0:T(8,128)S(1)}, f32[8,384]{1,0:T(8,128)S(1)}, f32[384,8,128]{2,0,1:T(8,128)S(1)}) conditional(s32[]{:T(128)} %convert_element_type.65, (s32[]{:T(128)}, s32[512]{0:T(512)S(1)}, s32[]{:T(128)}, bf16[3072,1024]{0,1:T(8,128)(2,1)}, bf16[384,8,128]{2,0,1:T(8,128)(2,1)S(1)}, /*index=5*/f32[8,384]{1,0:T(8,128)S(1)}, ...), branch_computations={%region_2.4_spmd, %region_5.5_spmd} | conditional | flops 823601024 | bytes 30067270 | solution.py:97
  567.8 7.3 %conditional.3 = (f32[8,384]{1,0:T(8,128)S(1)}, f32[8,384]{1,0:T(8,128)S(1)}, f32[384,8,128]{2,0,1:T(8,128)S(1)}) conditional(s32[]{:T(128)} %convert_element_type.65, (s32[]{:T(128)}, s32[512]{0:T(512)S(1)}, s32[]{:T(128)}, bf16[3072,1024]{0,1:T(8,128)(2,1)}, bf16[384,8,128]{2,0,1:T(8,128)(2,1)S(1)}, /*index=5*/f32[8,384]{1,0:T(8,128)S(1)}, ...), branch_computations={%region_2.4_spmd, %region_5.5_spmd} | conditional | flops 823601024 | bytes 30067270 | solution.py:97
  575.7 7.3 %conditional.3 = (f32[8,384]{1,0:T(8,128)S(1)}, f32[8,384]{1,0:T(8,128)S(1)}, f32[384,8,128]{2,0,1:T(8,128)S(1)}) conditional(s32[]{:T(128)} %convert_element_type.65, (s32[]{:T(128)}, s32[512]{0:T(512)S(1)}, s32[]{:T(128)}, bf16[3072,1024]{0,1:T(8,128)(2,1)}, bf16[384,8,128]{2,0,1:T(8,128)(2,1)S(1)}, /*index=5*/f32[8,384]{1,0:T(8,128)S(1)}, ...), branch_computations={%region_2.4_spmd, %region_5.5_spmd} | conditional | flops 823601024 | bytes 30067270 | solution.py:97
  583.6 5.7 psum.7
  (150 shorter events, 104.8 us)
Async XLA Ops:
  6.5 528.6 %all-gather.2.cloned.1.call-start = ((), (), s32[]{:S(2)}) async-start(), calls=%async_computation | async-start | bytes 7077888 | tf_op jit(solution)/shard_map/all_gather | solution.py:54
  7.7 264.1 %collective-permute-start = (bf16[3,128,1024]{2,1,0:T(8,128)(2,1)S(1)}, bf16[3,128,1024]{2,1,0:T(8,128)(2,1)}, u32[]{:S(2)}, u32[]{:S(2)}) collective-permute-start(bf16[3,128,1024]{2,1,0:T(8,128)(2,1)S(1)} %slice.21), channel_id=1, source_target_pairs={{0,4},{4,8},{8,12},{12,16},{16,20},{20,24},{24,28},{1,5},{5,9},{9,... | collective-permute-start | bytes 2359304 | tf_op jit(solution)/shard_map/ppermute | solution.py:15
  125.2 17.3 %copy-start.8 = (s32[16384]{0:T(1024)S(1)}, s32[16384]{0:T(1024)}, u32[]{:S(2)}) copy-start(s32[16384]{0:T(1024)} %constant.121) | copy-start | bytes 196612
  276.9 13.7 %slice-start.2 = ((s8[6291456]{0:T(1024)(128)(4,1)}), s8[2097152]{0:T(1024)(128)(4,1)S(1)}, s32[]{:S(2)}) async-start(s8[6291456]{0:T(1024)(128)(4,1)} %bitcast.78), calls=%async_computation.3 | async-start | bytes 4194304
  282.5 8.1 %slice-start.3 = ((s8[6291456]{0:T(1024)(128)(4,1)}), s8[4194304]{0:T(1024)(128)(4,1)S(1)}, s32[]{:S(2)}) async-start(s8[6291456]{0:T(1024)(128)(4,1)} %bitcast.78), calls=%async_computation.4 | async-start | bytes 8388608
  282.5 8.1 %copy-start.7 = (pred[128,128]{1,0:T(32,128)(4,1)S(1)}, pred[128,128]{1,0:T(32,128)(4,1)}, u32[]{:S(2)}) copy-start(pred[128,128]{1,0:T(32,128)(4,1)} %constant.118.clone) | copy-start | bytes 49156
  282.5 14.2 %slice-start = ((s8[6291456]{0:T(1024)(128)(4,1)}), s8[4194304]{0:T(1024)(128)(4,1)S(1)}, s32[]{:S(2)}) async-start(s8[6291456]{0:T(1024)(128)(4,1)} %bitcast.76), calls=%async_computation.1 | async-start | bytes 8388608
  290.6 6.1 %slice-start.1 = ((s8[6291456]{0:T(1024)(128)(4,1)}), s8[2097152]{0:T(1024)(128)(4,1)S(1)}, s32[]{:S(2)}) async-start(s8[6291456]{0:T(1024)(128)(4,1)} %bitcast.76), calls=%async_computation.2 | async-start | bytes 4194304
  290.6 6.1 %copy-start.6 = (pred[128,128]{1,0:T(32,128)(4,1)S(1)}, pred[128,128]{1,0:T(32,128)(4,1)}, u32[]{:S(2)}) copy-start(pred[128,128]{1,0:T(32,128)(4,1)} %constant.116.clone) | copy-start | bytes 49156
  308.2 164.2 %copy-start.4 = (bf16[384,1024]{0,1:T(8,128)(2,1)}, bf16[384,1024]{0,1:T(8,128)(2,1)S(1)}, u32[]{:S(2)}) copy-start(bf16[384,1024]{0,1:T(8,128)(2,1)S(1)} %get-tuple-element.347) | copy-start | bytes 2359300
  308.2 27.4 %collective-permute-start.1 = (bf16[384,1024]{0,1:T(8,128)(2,1)S(1)}, bf16[384,1024]{0,1:T(8,128)(2,1)S(1)}, u32[]{:S(2)}, u32[]{:S(2)}) collective-permute-start(bf16[384,1024]{0,1:T(8,128)(2,1)S(1)} %get-tuple-element.347), channel_id=1, source_target_pairs={{0,28},{4,0},{8,4},{12,8},{16,12},{20,16},{24,20},{28,24},{1,29},{... | collective-permute-start | bytes 2359304 | tf_op jit(solution)/shard_map/ppermute | solution.py:59
  335.6 33.2 %collective-permute-start.2 = (bf16[384,1024]{0,1:T(8,128)(2,1)S(1)}, bf16[384,1024]{0,1:T(8,128)(2,1)S(1)}, u32[]{:S(2)}, u32[]{:S(2)}) collective-permute-start(bf16[384,1024]{0,1:T(8,128)(2,1)S(1)} %collective-permute-done.1), channel_id=1, source_target_pairs={{0,28},{4,0},{8,4},{12,8},{16,12},{20,16},{24,20},{28,24},{1,29},{... | collective-permute-start | bytes 2359304 | tf_op jit(solution)/shard_map/ppermute | solution.py:59
  368.8 35.5 %collective-permute-start.3 = (bf16[384,1024]{0,1:T(8,128)(2,1)S(1)}, bf16[384,1024]{0,1:T(8,128)(2,1)S(1)}, u32[]{:S(2)}, u32[]{:S(2)}) collective-permute-start(bf16[384,1024]{0,1:T(8,128)(2,1)S(1)} %collective-permute-done.2), channel_id=1, source_target_pairs={{0,28},{4,0},{8,4},{12,8},{16,12},{20,16},{24,20},{28,24},{1,29},{... | collective-permute-start | bytes 2359304 | tf_op jit(solution)/shard_map/ppermute | solution.py:59
  404.3 0.9 copy-start
  405.2 34.3 %collective-permute-start.4 = (bf16[384,1024]{0,1:T(8,128)(2,1)S(1)}, bf16[384,1024]{0,1:T(8,128)(2,1)S(1)}, u32[]{:S(2)}, u32[]{:S(2)}) collective-permute-start(bf16[384,1024]{0,1:T(8,128)(2,1)S(1)} %collective-permute-done.3), channel_id=1, source_target_pairs={{0,28},{4,0},{8,4},{12,8},{16,12},{20,16},{24,20},{28,24},{1,29},{... | collective-permute-start | bytes 2359304 | tf_op jit(solution)/shard_map/ppermute | solution.py:59
  439.5 0.9 copy-start.2
  440.4 32.0 %collective-permute-start.5 = (bf16[384,1024]{0,1:T(8,128)(2,1)S(1)}, bf16[384,1024]{0,1:T(8,128)(2,1)}, u32[]{:S(2)}, u32[]{:S(2)}) collective-permute-start(bf16[384,1024]{0,1:T(8,128)(2,1)S(1)} %collective-permute-done.4), channel_id=1, source_target_pairs={{0,28},{4,0},{8,4},{12,8},{16,12},{20,16},{24,20},{28,24},{1,29},{... | collective-permute-start | bytes 2359304 | tf_op jit(solution)/shard_map/ppermute | solution.py:59
  472.4 22.1 %collective-permute-start.6 = (bf16[384,1024]{0,1:T(8,128)(2,1)}, bf16[384,1024]{0,1:T(8,128)(2,1)}, u32[]{:S(2)}, u32[]{:S(2)}) collective-permute-start(bf16[384,1024]{0,1:T(8,128)(2,1)} %collective-permute-done.5), channel_id=1, source_target_pairs={{0,28},{4,0},{8,4},{12,8},{16,12},{20,16},{24,20},{28,24},{1,29},{... | collective-permute-start | bytes 2359304 | tf_op jit(solution)/shard_map/ppermute | solution.py:59
  478.2 37.6 %copy-start.5 = (bf16[384,1024]{0,1:T(8,128)(2,1)S(1)}, bf16[384,1024]{0,1:T(8,128)(2,1)}, u32[]{:S(2)}) copy-start(bf16[384,1024]{0,1:T(8,128)(2,1)} %copy-done.4) | copy-start | bytes 2359300
  494.5 20.3 %collective-permute-start.7 = (bf16[384,1024]{0,1:T(8,128)(2,1)}, bf16[384,1024]{0,1:T(8,128)(2,1)S(1)}, u32[]{:S(2)}, u32[]{:S(2)}) collective-permute-start(bf16[384,1024]{0,1:T(8,128)(2,1)} %collective-permute-done.6), channel_id=1, source_target_pairs={{0,28},{4,0},{8,4},{12,8},{16,12},{20,16},{24,20},{28,24},{1,29},{... | collective-permute-start | bytes 2359304 | tf_op jit(solution)/shard_map/ppermute | solution.py:59
  497.0 22.0 %copy-start.1 = (bf16[384,1024]{0,1:T(8,128)(2,1)S(1)}, bf16[384,1024]{0,1:T(8,128)(2,1)}, u32[]{:S(2)}) copy-start(bf16[384,1024]{0,1:T(8,128)(2,1)} %copy-done) | copy-start | bytes 2359300
  499.3 20.8 %copy-start.3 = (bf16[384,1024]{0,1:T(8,128)(2,1)S(1)}, bf16[384,1024]{0,1:T(8,128)(2,1)}, u32[]{:S(2)}) copy-start(bf16[384,1024]{0,1:T(8,128)(2,1)} %copy-done.2) | copy-start | bytes 2359300
  535.3 54.0 %copy-start.9 = (f32[1024]{0:T(1024)S(1)}, f32[1024]{0:T(1024)}, u32[]{:S(2)}) copy-start(f32[1024]{0:T(1024)} %param.15) | copy-start | bytes 12292
Sparse Core Ops, SparseCore 0:
  306.6 170.1 all-gather.1
